TPU v7x, 32 devices: a whole 2x2x4 slice. The times are simulated.
32 devices in a mesh: groups: 2 (over y), rows: 4 (over z), cols: 2 (over x), sub: 2 (over core).
Axes of the slice: x: 2, y: 2, z: 4, core: 2. Of those that a mesh axis runs over, the one named last changes fastest.
Arguments:
- elevation: float32 [256, 16384], P(('groups', 'rows', 'sub'), 'cols'), parts along dimension 0, may hold values from -6 to 6
- fill_depth: float32 [256, 16384], P(('groups', 'rows', 'sub'), 'cols'), parts along dimension 0, may hold values from 0.5 to 4
- edge_rows: int32 [4, 16384], P('groups', 'cols'), parts along dimension 0, may hold values 0 or 1
- edge_sides: int32 [4, 128], P('groups', ('rows', 'sub')), parts along dimension 0, may hold values 0 or 1
- adjacency: int32 [16, 6], P('groups'), parts along dimension 0, may hold values from 0 to 7
Outputs:
- filled: float32 [256, 16384], P(('groups', 'rows', 'sub'), 'cols'), parts along dimension 0
There are 2 independent parts, one for each index of `groups`. A program takes and returns all parts, laid end to end along the dimension named above; each array names one. Nothing has to cross between parts.
Inputs may be any that keep to these rules, and one draw needn't show every extreme that they name: `adjacency`: tile numbers count tiles row by row.
All inputs are finite; a program needn't handle non-finite values. No bound on the sum of `edge_rows` or of `edge_sides` on one device may be relied on, other than what follows from the above.
Results may differ from a plain program's by a relative error of at most 0.00002.
Values sent between devices are 32-bit elements; how exact they have to be, the bound alone decides.
A program may use at most 64 MiB of HBM per device.

v0:
```python
import jax
import jax.numpy as jnp
from jax import lax
from jax.sharding import PartitionSpec as P

PASSES = 8
ROUNDS = 4


unreached = 1000000000.0
rise_step = 0.01
hop_rise = 0.05
spill_lift = 3.0


def with_halo(block, sides, width):
    for axis, dim in sides:
        count = lax.axis_size(axis)
        forward = [(i, i + 1) for i in range(count - 1)]
        backward = [(target, source) for source, target in forward]
        low = lax.ppermute(
            lax.slice_in_dim(block, block.shape[dim] - width, None, axis=dim), axis, forward
        )
        high = lax.ppermute(lax.slice_in_dim(block, 0, width, axis=dim), axis, backward)
        block = jnp.concatenate([low, block, high], axis=dim)
    return block


def neighbour_min(padded):
    height = padded.shape[0] - 2
    width = padded.shape[1] - 2
    lowest = None
    for shift_row in range(3):
        for shift_col in range(3):
            if shift_row == 1 and shift_col == 1:
                continue
            piece = padded[shift_row : shift_row + height, shift_col : shift_col + width]
            lowest = piece if lowest is None else jnp.minimum(lowest, piece)
    return lowest


def outside_mask(height, width, margin):
    row_first = lax.axis_index(("rows", "sub")) * height - margin
    col_first = lax.axis_index("cols") * width - margin
    grid_rows = lax.axis_size(("rows", "sub")) * height
    grid_cols = lax.axis_size("cols") * width
    global_rows = row_first + jnp.arange(height + 2 * margin, dtype=jnp.int32)
    global_cols = col_first + jnp.arange(width + 2 * margin, dtype=jnp.int32)
    row_out = (global_rows < 0) | (global_rows >= grid_rows)
    col_out = (global_cols < 0) | (global_cols >= grid_cols)
    return row_out[:, None] | col_out[None, :]


def relax_deep(surface, ground_wide, outside_wide):
    current = with_halo(surface, ((("rows", "sub"), 0), ("cols", 1)), 4)
    current = jnp.where(outside_wide, unreached, current)
    for step in range(4):
        cut = step + 1
        lowest = neighbour_min(current)
        inner = current[1:-1, 1:-1]
        ground_part = ground_wide[cut:-cut, cut:-cut]
        updated = jnp.maximum(ground_part, jnp.minimum(inner, lowest + rise_step))
        current = jnp.where(outside_wide[cut:-cut, cut:-cut], unreached, updated)
    return current


def lookup_min(levels, links):
    count = levels.shape[0]
    matches = links[..., None] == jnp.arange(count, dtype=jnp.int32)
    return jnp.min(jnp.where(matches, levels, unreached), axis=-1)


def per_device(elevation, fill_depth, edge_rows, edge_sides, adjacency):
    height, width = elevation.shape
    row_index = lax.axis_index(("rows", "sub"))
    col_index = lax.axis_index("cols")
    grid_rows = lax.axis_size(("rows", "sub")) * height
    grid_cols = lax.axis_size("cols") * width
    global_rows = row_index * height + jnp.arange(height, dtype=jnp.int32)
    global_cols = col_index * width + jnp.arange(width, dtype=jnp.int32)
    outlet = (global_rows[:, None] == 0) & (edge_rows[0][None, :] == 1)
    outlet = outlet | (global_rows[:, None] == grid_rows - 1) & (edge_rows[1][None, :] == 1)
    outlet = outlet | (global_cols[None, :] == 0) & (edge_sides[0][:, None] == 1)
    outlet = outlet | (global_cols[None, :] == grid_cols - 1) & (edge_sides[1][:, None] == 1)
    surface = jnp.where(outlet, elevation, elevation + fill_depth)
    outside_wide = outside_mask(height, width, 4)
    ground_wide = with_halo(elevation, ((("rows", "sub"), 0), ("cols", 1)), 4)
    for step in range(PASSES // 4):
        surface = relax_deep(surface, ground_wide, outside_wide)
    sub_index = lax.axis_index("sub")
    sub_count = lax.axis_size("sub")
    floor_local = jnp.minimum(jnp.min(surface[:, 0]), jnp.min(surface[:, -1]))
    floor_local = jnp.minimum(
        floor_local, jnp.where(sub_index == 0, jnp.min(surface[0]), unreached)
    )
    floor_local = jnp.minimum(
        floor_local, jnp.where(sub_index == sub_count - 1, jnp.min(surface[-1]), unreached)
    )
    level = lax.pmin(floor_local, "sub")
    tile_id = lax.axis_index("rows") * lax.axis_size("cols") + col_index
    tile_count = adjacency.shape[0]
    tile_ids = jnp.arange(tile_count, dtype=jnp.int32)
    own_links = jnp.sum(jnp.where(tile_ids[:, None] == tile_id, adjacency, 0), axis=0)
    for step in range(ROUNDS):
        every = lax.all_gather(level[None], ("rows", "cols"), axis=0, tiled=True)
        level = jnp.minimum(level, jnp.min(lookup_min(every, own_links)) + hop_rise)
    surface = jnp.maximum(elevation, jnp.minimum(surface, level + spill_lift))
    surface = relax_deep(surface, ground_wide, outside_wide)
    return surface


def solution(mesh):
    placed = (
        P(("groups", "rows", "sub"), "cols"),
        P(("groups", "rows", "sub"), "cols"),
        P("groups", "cols"),
        P("groups", ("rows", "sub")),
        P("groups", None),
    )
    return jax.shard_map(
        per_device,
        mesh=mesh,
        in_specs=placed,
        out_specs=P(("groups", "rows", "sub"), "cols"),
        check_vma=False,
    )
```

profile of v0, /device:TPU:1, one launch (start us, length us, event | category | flops | bytes accessed | tf_op | source)
XLA Modules:
  0.0 174.8 jit_solution(8688255670115900465)
XLA Ops:
  2.7 4.7 %collective-permute-start.4 = (f32[4,8192]{1,0:T(4,128)S(1)}, f32[4,8192]{1,0:T(4,128)S(1)}, u32[]{:S(2)}, u32[]{:S(2)}) collective-permute-start(f32[4,8192]{1,0:T(4,128)S(1)} %get-tuple-element.25), channel_id=1, source_target_pairs={{0,1},{1,4},{4,5},{5,8},{8,9},{9,12},{12,13},{2,3},{3,6},{6,7},{7,... | collective-permute-start | bytes 393224 | tf_op jit(solution)/shard_map/ppermute | solution.py:21
  7.5 1.9 %collective-permute-start.5 = (f32[4,8192]{1,0:T(4,128)S(1)}, f32[4,8192]{1,0:T(4,128)S(1)}, u32[]{:S(2)}, u32[]{:S(2)}) collective-permute-start(f32[4,8192]{1,0:T(4,128)S(1)} %get-tuple-element.26), channel_id=1, source_target_pairs={{1,0},{4,1},{5,4},{8,5},{9,8},{12,9},{13,12},{3,2},{6,3},{7,6},{10... | collective-permute-start | bytes 393224 | tf_op jit(solution)/shard_map/ppermute | solution.py:24
  9.5 3.6 %collective-permute-start = (f32[4,8192]{1,0:T(4,128)S(1)}, f32[4,8192]{1,0:T(4,128)S(1)}, u32[]{:S(2)}, u32[]{:S(2)}) collective-permute-start(f32[4,8192]{1,0:T(4,128)S(1)} %get-tuple-element.23), channel_id=1, source_target_pairs={{0,1},{1,4},{4,5},{5,8},{8,9},{9,12},{12,13},{2,3},{3,6},{6,7},{7,... | collective-permute-start | bytes 393224 | tf_op jit(solution)/shard_map/ppermute | solution.py:21
  13.1 1.9 %collective-permute-start.1 = (f32[4,8192]{1,0:T(4,128)S(1)}, f32[4,8192]{1,0:T(4,128)S(1)}, u32[]{:S(2)}, u32[]{:S(2)}) collective-permute-start(f32[4,8192]{1,0:T(4,128)S(1)} %get-tuple-element.24), channel_id=1, source_target_pairs={{1,0},{4,1},{5,4},{8,5},{9,8},{12,9},{13,12},{3,2},{6,3},{7,6},{10... | collective-permute-start | bytes 393224 | tf_op jit(solution)/shard_map/ppermute | solution.py:24
  15.5 3.1 %collective-permute-start.6 = (f32[24,4]{1,0:T(8,128)S(1)}, f32[24,4]{1,0:T(8,128)S(1)}, u32[]{:S(2)}, u32[]{:S(2)}) collective-permute-start(f32[24,4]{1,0:T(8,128)S(1)} %get-tuple-element.18), channel_id=1, source_target_pairs={{0,2},{1,3},{4,6},{5,7},{8,10},{9,11},{12,14},{13,15},{16,18},{17,... | collective-permute-start | bytes 1160 | tf_op jit(solution)/shard_map/ppermute | solution.py:21
  20.1 4.0 %collective-permute-start.2 = (f32[24,4]{1,0:T(8,128)S(1)}, f32[24,4]{1,0:T(8,128)S(1)}, u32[]{:S(2)}, u32[]{:S(2)}) collective-permute-start(f32[24,4]{1,0:T(8,128)S(1)} %get-tuple-element.16), channel_id=1, source_target_pairs={{0,2},{1,3},{4,6},{5,7},{8,10},{9,11},{12,14},{13,15},{16,18},{17,... | collective-permute-start | bytes 1160 | tf_op jit(solution)/shard_map/ppermute | solution.py:21
  29.0 1.7 fusion.35
  35.2 5.6 %collective-permute-start.8 = (f32[4,8192]{1,0:T(4,128)S(1)}, f32[4,8192]{1,0:T(4,128)S(1)}, u32[]{:S(2)}, u32[]{:S(2)}) collective-permute-start(f32[4,8192]{1,0:T(4,128)S(1)} %get-tuple-element.21), channel_id=1, source_target_pairs={{0,1},{1,4},{4,5},{5,8},{8,9},{9,12},{12,13},{2,3},{3,6},{6,7},{7,... | collective-permute-start | bytes 393224 | tf_op jit(solution)/shard_map/ppermute | solution.py:21
  40.9 1.9 %collective-permute-start.9 = (f32[4,8192]{1,0:T(4,128)S(1)}, f32[4,8192]{1,0:T(4,128)S(1)}, u32[]{:S(2)}, u32[]{:S(2)}) collective-permute-start(f32[4,8192]{1,0:T(4,128)S(1)} %get-tuple-element.22), channel_id=1, source_target_pairs={{1,0},{4,1},{5,4},{8,5},{9,8},{12,9},{13,12},{3,2},{6,3},{7,6},{10... | collective-permute-start | bytes 393224 | tf_op jit(solution)/shard_map/ppermute | solution.py:24
  42.8 4.3 %collective-permute-done.9 = f32[4,8192]{1,0:T(4,128)S(1)} collective-permute-done((f32[4,8192]{1,0:T(4,128)S(1)}, f32[4,8192]{1,0:T(4,128)S(1)}, u32[]{:S(2)}, u32[]{:S(2)}) %collective-permute-start.9) | collective-permute-done | bytes 131104 | tf_op jit(solution)/shard_map/ppermute | solution.py:24
  47.3 2.5 %collective-permute-start.10 = (f32[24,4]{1,0:T(8,128)S(1)}, f32[24,4]{1,0:T(8,128)S(1)}, u32[]{:S(2)}, u32[]{:S(2)}) collective-permute-start(f32[24,4]{1,0:T(8,128)S(1)} %get-tuple-element.14), channel_id=1, source_target_pairs={{0,2},{1,3},{4,6},{5,7},{8,10},{9,11},{12,14},{13,15},{16,18},{17,... | collective-permute-start | bytes 1160 | tf_op jit(solution)/shard_map/ppermute | solution.py:21
  51.3 2.9 %collective-permute-done.11 = f32[24,4]{1,0:T(8,128)S(1)} collective-permute-done((f32[24,4]{1,0:T(8,128)S(1)}, f32[24,4]{1,0:T(8,128)S(1)}, u32[]{:S(2)}, u32[]{:S(2)}) %collective-permute-start.11) | collective-permute-done | bytes 416 | tf_op jit(solution)/shard_map/ppermute | solution.py:24
  56.5 1.7 fusion.19
  66.3 3.0 %pmin.7 = f32[]{:T(128)} all-reduce(f32[]{:T(128)S(6)} %min.383), channel_id=1, replica_groups=mesh['groups'=2,'rows'=4,'cols'=2,'sub'=2] {'sub'}, use_global_device_ids=true, to_apply=%region_4.5 | all-reduce | flops 1 | bytes 8 | tf_op jit(solution)/shard_map/pmin | solution.py:99
  70.8 15.9 %all-reduce = f32[8]{0:T(128)S(1)} all-reduce(f32[8]{0:T(128)S(1)} %dynamic-update-slice), channel_id=1, replica_groups=mesh['groups'=2,'rows'=4,'cols'=2,'sub'=2] {'rows','cols'}, use_global_device_ids=true, to_apply=%add | all-reduce | flops 8 | bytes 64
  89.4 13.7 %all-reduce.1 = f32[8]{0:T(128)S(1)} all-reduce(f32[8]{0:T(128)S(1)} %dynamic-update-slice.1), channel_id=1, replica_groups=mesh['groups'=2,'rows'=4,'cols'=2,'sub'=2] {'rows','cols'}, use_global_device_ids=true, to_apply=%add.1 | all-reduce | flops 8 | bytes 64
  105.1 15.3 %all-reduce.2 = f32[8]{0:T(128)S(1)} all-reduce(f32[8]{0:T(128)S(1)} %dynamic-update-slice.2), channel_id=1, replica_groups=mesh['groups'=2,'rows'=4,'cols'=2,'sub'=2] {'rows','cols'}, use_global_device_ids=true, to_apply=%add.2 | all-reduce | flops 8 | bytes 64
  122.5 13.7 %all-reduce.3 = f32[8]{0:T(128)S(1)} all-reduce(f32[8]{0:T(128)S(1)} %dynamic-update-slice.3), channel_id=1, replica_groups=mesh['groups'=2,'rows'=4,'cols'=2,'sub'=2] {'rows','cols'}, use_global_device_ids=true, to_apply=%add.3 | all-reduce | flops 8 | bytes 64
  137.8 15.0 %collective-permute-start.12 = (f32[4,8192]{1,0:T(4,128)S(1)}, f32[4,8192]{1,0:T(4,128)S(1)}, u32[]{:S(2)}, u32[]{:S(2)}) collective-permute-start(f32[4,8192]{1,0:T(4,128)S(1)} %get-tuple-element.19), channel_id=1, source_target_pairs={{0,1},{1,4},{4,5},{5,8},{8,9},{9,12},{12,13},{2,3},{3,6},{6,7},{7,... | collective-permute-start | bytes 393224 | tf_op jit(solution)/shard_map/ppermute | solution.py:21
  152.8 2.9 %collective-permute-start.13 = (f32[4,8192]{1,0:T(4,128)S(1)}, f32[4,8192]{1,0:T(4,128)S(1)}, u32[]{:S(2)}, u32[]{:S(2)}) collective-permute-start(f32[4,8192]{1,0:T(4,128)S(1)} %get-tuple-element.20), channel_id=1, source_target_pairs={{1,0},{4,1},{5,4},{8,5},{9,8},{12,9},{13,12},{3,2},{6,3},{7,6},{10... | collective-permute-start | bytes 393224 | tf_op jit(solution)/shard_map/ppermute | solution.py:24
  155.7 3.3 %collective-permute-done.13 = f32[4,8192]{1,0:T(4,128)S(1)} collective-permute-done((f32[4,8192]{1,0:T(4,128)S(1)}, f32[4,8192]{1,0:T(4,128)S(1)}, u32[]{:S(2)}, u32[]{:S(2)}) %collective-permute-start.13) | collective-permute-done | bytes 131104 | tf_op jit(solution)/shard_map/ppermute | solution.py:24
  159.2 3.6 %collective-permute-start.14 = (f32[24,4]{1,0:T(8,128)S(1)}, f32[24,4]{1,0:T(8,128)S(1)}, u32[]{:S(2)}, u32[]{:S(2)}) collective-permute-start(f32[24,4]{1,0:T(8,128)S(1)} %get-tuple-element.12), channel_id=1, source_target_pairs={{0,2},{1,3},{4,6},{5,7},{8,10},{9,11},{12,14},{13,15},{16,18},{17,... | collective-permute-start | bytes 1160 | tf_op jit(solution)/shard_map/ppermute | solution.py:21
  164.4 2.9 %collective-permute-done.15 = f32[24,4]{1,0:T(8,128)S(1)} collective-permute-done((f32[24,4]{1,0:T(8,128)S(1)}, f32[24,4]{1,0:T(8,128)S(1)}, u32[]{:S(2)}, u32[]{:S(2)}) %collective-permute-start.15) | collective-permute-done | bytes 416 | tf_op jit(solution)/shard_map/ppermute | solution.py:24
  173.0 1.8 %fusion.39 = f32[16,8192]{1,0:T(8,128)} fusion(f32[16,8192]{1,0:T(8,128)S(1)} %copy-done, f32[18,8194]{1,0:T(8,128)S(1)} %fusion.3, pred[24,8200]{1,0:T(8,128)(4,1)S(1)} %broadcast_or_fusion), kind=kLoop, calls=%fused_computation.111 | loop fusion | flops 1441792 | bytes 5898240 | tf_op jit(solution)/shard_map/jit(_where)/select_n | solution.py:63
  (78 shorter events, 37.5 us)
Async XLA Ops:
  0.0 1.1 copy-start.2
  2.7 6.7 %copy-start = (f32[16,8192]{1,0:T(8,128)S(1)}, f32[16,8192]{1,0:T(8,128)}, u32[]{:S(2)}) copy-start(f32[16,8192]{1,0:T(8,128)} %param.5) | copy-start | bytes 1572868
  2.7 12.5 %collective-permute-start.4 = (f32[4,8192]{1,0:T(4,128)S(1)}, f32[4,8192]{1,0:T(4,128)S(1)}, u32[]{:S(2)}, u32[]{:S(2)}) collective-permute-start(f32[4,8192]{1,0:T(4,128)S(1)} %get-tuple-element.25), channel_id=1, source_target_pairs={{0,1},{1,4},{4,5},{5,8},{8,9},{9,12},{12,13},{2,3},{3,6},{6,7},{7,... | collective-permute-start | bytes 393224 | tf_op jit(solution)/shard_map/ppermute | solution.py:21
  7.5 7.8 %collective-permute-start.5 = (f32[4,8192]{1,0:T(4,128)S(1)}, f32[4,8192]{1,0:T(4,128)S(1)}, u32[]{:S(2)}, u32[]{:S(2)}) collective-permute-start(f32[4,8192]{1,0:T(4,128)S(1)} %get-tuple-element.26), channel_id=1, source_target_pairs={{1,0},{4,1},{5,4},{8,5},{9,8},{12,9},{13,12},{3,2},{6,3},{7,6},{10... | collective-permute-start | bytes 393224 | tf_op jit(solution)/shard_map/ppermute | solution.py:24
  9.5 10.4 %collective-permute-start = (f32[4,8192]{1,0:T(4,128)S(1)}, f32[4,8192]{1,0:T(4,128)S(1)}, u32[]{:S(2)}, u32[]{:S(2)}) collective-permute-start(f32[4,8192]{1,0:T(4,128)S(1)} %get-tuple-element.23), channel_id=1, source_target_pairs={{0,1},{1,4},{4,5},{5,8},{8,9},{9,12},{12,13},{2,3},{3,6},{6,7},{7,... | collective-permute-start | bytes 393224 | tf_op jit(solution)/shard_map/ppermute | solution.py:21
  13.1 6.8 %collective-permute-start.1 = (f32[4,8192]{1,0:T(4,128)S(1)}, f32[4,8192]{1,0:T(4,128)S(1)}, u32[]{:S(2)}, u32[]{:S(2)}) collective-permute-start(f32[4,8192]{1,0:T(4,128)S(1)} %get-tuple-element.24), channel_id=1, source_target_pairs={{1,0},{4,1},{5,4},{8,5},{9,8},{12,9},{13,12},{3,2},{6,3},{7,6},{10... | collective-permute-start | bytes 393224 | tf_op jit(solution)/shard_map/ppermute | solution.py:24
  15.5 9.9 %collective-permute-start.6 = (f32[24,4]{1,0:T(8,128)S(1)}, f32[24,4]{1,0:T(8,128)S(1)}, u32[]{:S(2)}, u32[]{:S(2)}) collective-permute-start(f32[24,4]{1,0:T(8,128)S(1)} %get-tuple-element.18), channel_id=1, source_target_pairs={{0,2},{1,3},{4,6},{5,7},{8,10},{9,11},{12,14},{13,15},{16,18},{17,... | collective-permute-start | bytes 1160 | tf_op jit(solution)/shard_map/ppermute | solution.py:21
  18.6 6.8 %collective-permute-start.7 = (f32[24,4]{1,0:T(8,128)S(1)}, f32[24,4]{1,0:T(8,128)S(1)}, u32[]{:S(2)}, u32[]{:S(2)}) collective-permute-start(f32[24,4]{1,0:T(8,128)S(1)} %get-tuple-element.17), channel_id=1, source_target_pairs={{2,0},{3,1},{6,4},{7,5},{10,8},{11,9},{14,12},{15,13},{18,16},{19,... | collective-permute-start | bytes 1160 | tf_op jit(solution)/shard_map/ppermute | solution.py:24
  20.1 7.8 %collective-permute-start.2 = (f32[24,4]{1,0:T(8,128)S(1)}, f32[24,4]{1,0:T(8,128)S(1)}, u32[]{:S(2)}, u32[]{:S(2)}) collective-permute-start(f32[24,4]{1,0:T(8,128)S(1)} %get-tuple-element.16), channel_id=1, source_target_pairs={{0,2},{1,3},{4,6},{5,7},{8,10},{9,11},{12,14},{13,15},{16,18},{17,... | collective-permute-start | bytes 1160 | tf_op jit(solution)/shard_map/ppermute | solution.py:21
  24.1 4.4 %collective-permute-start.3 = (f32[24,4]{1,0:T(8,128)S(1)}, f32[24,4]{1,0:T(8,128)S(1)}, u32[]{:S(2)}, u32[]{:S(2)}) collective-permute-start(f32[24,4]{1,0:T(8,128)S(1)} %get-tuple-element.15), channel_id=1, source_target_pairs={{2,0},{3,1},{6,4},{7,5},{10,8},{11,9},{14,12},{15,13},{18,16},{19,... | collective-permute-start | bytes 1160 | tf_op jit(solution)/shard_map/ppermute | solution.py:24
  35.2 7.6 %collective-permute-start.8 = (f32[4,8192]{1,0:T(4,128)S(1)}, f32[4,8192]{1,0:T(4,128)S(1)}, u32[]{:S(2)}, u32[]{:S(2)}) collective-permute-start(f32[4,8192]{1,0:T(4,128)S(1)} %get-tuple-element.21), channel_id=1, source_target_pairs={{0,1},{1,4},{4,5},{5,8},{8,9},{9,12},{12,13},{2,3},{3,6},{6,7},{7,... | collective-permute-start | bytes 393224 | tf_op jit(solution)/shard_map/ppermute | solution.py:21
  40.9 6.3 %collective-permute-start.9 = (f32[4,8192]{1,0:T(4,128)S(1)}, f32[4,8192]{1,0:T(4,128)S(1)}, u32[]{:S(2)}, u32[]{:S(2)}) collective-permute-start(f32[4,8192]{1,0:T(4,128)S(1)} %get-tuple-element.22), channel_id=1, source_target_pairs={{1,0},{4,1},{5,4},{8,5},{9,8},{12,9},{13,12},{3,2},{6,3},{7,6},{10... | collective-permute-start | bytes 393224 | tf_op jit(solution)/shard_map/ppermute | solution.py:24
  47.3 4.0 %collective-permute-start.10 = (f32[24,4]{1,0:T(8,128)S(1)}, f32[24,4]{1,0:T(8,128)S(1)}, u32[]{:S(2)}, u32[]{:S(2)}) collective-permute-start(f32[24,4]{1,0:T(8,128)S(1)} %get-tuple-element.14), channel_id=1, source_target_pairs={{0,2},{1,3},{4,6},{5,7},{8,10},{9,11},{12,14},{13,15},{16,18},{17,... | collective-permute-start | bytes 1160 | tf_op jit(solution)/shard_map/ppermute | solution.py:21
  49.8 4.4 %collective-permute-start.11 = (f32[24,4]{1,0:T(8,128)S(1)}, f32[24,4]{1,0:T(8,128)S(1)}, u32[]{:S(2)}, u32[]{:S(2)}) collective-permute-start(f32[24,4]{1,0:T(8,128)S(1)} %get-tuple-element.13), channel_id=1, source_target_pairs={{2,0},{3,1},{6,4},{7,5},{10,8},{11,9},{14,12},{15,13},{18,16},{19,... | collective-permute-start | bytes 1160 | tf_op jit(solution)/shard_map/ppermute | solution.py:24
  65.0 0.7 copy-start.3
  69.2 1.5 copy-start.1
  137.8 17.9 %collective-permute-start.12 = (f32[4,8192]{1,0:T(4,128)S(1)}, f32[4,8192]{1,0:T(4,128)S(1)}, u32[]{:S(2)}, u32[]{:S(2)}) collective-permute-start(f32[4,8192]{1,0:T(4,128)S(1)} %get-tuple-element.19), channel_id=1, source_target_pairs={{0,1},{1,4},{4,5},{5,8},{8,9},{9,12},{12,13},{2,3},{3,6},{6,7},{7,... | collective-permute-start | bytes 393224 | tf_op jit(solution)/shard_map/ppermute | solution.py:21
  152.8 6.3 %collective-permute-start.13 = (f32[4,8192]{1,0:T(4,128)S(1)}, f32[4,8192]{1,0:T(4,128)S(1)}, u32[]{:S(2)}, u32[]{:S(2)}) collective-permute-start(f32[4,8192]{1,0:T(4,128)S(1)} %get-tuple-element.20), channel_id=1, source_target_pairs={{1,0},{4,1},{5,4},{8,5},{9,8},{12,9},{13,12},{3,2},{6,3},{7,6},{10... | collective-permute-start | bytes 393224 | tf_op jit(solution)/shard_map/ppermute | solution.py:24
  159.2 5.1 %collective-permute-start.14 = (f32[24,4]{1,0:T(8,128)S(1)}, f32[24,4]{1,0:T(8,128)S(1)}, u32[]{:S(2)}, u32[]{:S(2)}) collective-permute-start(f32[24,4]{1,0:T(8,128)S(1)} %get-tuple-element.12), channel_id=1, source_target_pairs={{0,2},{1,3},{4,6},{5,7},{8,10},{9,11},{12,14},{13,15},{16,18},{17,... | collective-permute-start | bytes 1160 | tf_op jit(solution)/shard_map/ppermute | solution.py:21
  162.8 4.4 %collective-permute-start.15 = (f32[24,4]{1,0:T(8,128)S(1)}, f32[24,4]{1,0:T(8,128)S(1)}, u32[]{:S(2)}, u32[]{:S(2)}) collective-permute-start(f32[24,4]{1,0:T(8,128)S(1)} %get-tuple-element.11), channel_id=1, source_target_pairs={{2,0},{3,1},{6,4},{7,5},{10,8},{11,9},{14,12},{15,13},{18,16},{19,... | collective-permute-start | bytes 1160 | tf_op jit(solution)/shard_map/ppermute | solution.py:24
where the time goes:
time: 176 us; the launch traced here: 175 us
  blocking collectives  61.6 us (35%)
  starting transfers between devices  56.4 us (32%)
  other arithmetic  28.5 us (16%)
  waiting for transfers between devices  14.2 us (8%)
  local copies, waits for them, and re-layouts  8.01 us (5%)
  between operations  6.12 us (3%)
    unnamed x4, blocking collectives  58.7 us
    ppermute x8, starting transfers between devices, with_halo(): lax.ppermute(lax.slice_in_dim(block, block.shape[dim] - width, None, axis...  42.1 us
    select_n x12, other arithmetic, relax_deep(): current = jnp.where(outside_wide[cut:-cut, cut:-cut], unreached, updated)  19.3 us
    ppermute x8, starting transfers between devices, with_halo(): lax.ppermute(lax.slice_in_dim(block, 0, width, axis=dim), axis, backward)  14.3 us
    ppermute x8, waiting for transfers between devices, with_halo(): lax.ppermute(lax.slice_in_dim(block, 0, width, axis=dim), axis, backward)  14.2 us
    unnamed x17, local copies, waits for them, and re-layouts  5.19 us
  transfers between devices with their start and end apart: 16, of which 5 were waited for; matrix products, arithmetic and copies ran while one was open for 2% of the time, Pallas kernels for 0%

commit v1 on v0

v1 whole, which is shorter than its diff:
```python
import functools

import jax
import jax.numpy as jnp
from jax import lax
from jax.experimental import pallas as pl
from jax.experimental.pallas import tpu as pltpu
from jax.sharding import PartitionSpec as P

PASSES = 8
ROUNDS = 4

unreached = 1000000000.0
rise_step = 0.01
hop_rise = 0.05
spill_lift = 3.0

DEPTH = 4
SUBL = 8
TILE = 128
HALF = TILE // 2
MESH = pl.DeviceIdType.MESH


def kernel(
    sizes, elev_hbm, fill_hbm, edge_hbm, side_hbm, adj_hbm, out_hbm,
    ground, fill, first, second, third, ping, pong, done,
    edge, side, adj, ring_own, ring_low, ring_high,
    mine, gathered, hops, levels,
    load_sem, send_sem, recv_sem, level_send, level_recv, out_sem,
):
    n_groups, n_rows, n_cols, n_sub = sizes
    height, width = elev_hbm.shape
    chunk = width // SUBL
    lanes = chunk + TILE
    low, high = DEPTH, DEPTH + height
    total = height + 2 * DEPTH
    n_tiles = adj.shape[0]
    padded = mine.shape[1]
    members = n_rows * n_cols * n_sub

    group = lax.axis_index("groups")
    tile_row = lax.axis_index("rows")
    col = lax.axis_index("cols")
    sub = lax.axis_index("sub")
    band = tile_row * n_sub + sub
    bands = n_rows * n_sub
    me = (tile_row * n_cols + col) * n_sub + sub

    has = {-1: band > 0, 1: band < bands - 1, 0: True}
    has_col = {-1: col > 0, 1: col < n_cols - 1, 0: True}

    def both(dr, dc):
        if dr == 0:
            return has_col[dc]
        if dc == 0:
            return has[dr]
        return jnp.logical_and(has[dr], has_col[dc])

    def device(dr, dc):
        to_band = band + dr
        return (group, to_band // n_sub, col + dc, to_band % n_sub)

    loads = []
    for number, (src, dst, at) in enumerate(
        ((elev_hbm, ground, low), (fill_hbm, fill, 0), (edge_hbm, edge, 0))
    ):
        count = src.shape[0]
        for s in range(SUBL):
            pltpu.make_async_copy(
                src.at[:, pl.ds(s * chunk, chunk)],
                dst.at[pl.ds(at, count), s, pl.ds(0, chunk)],
                load_sem.at[number],
            ).start()
        whole = dst.at[pl.ds(at, count), :, pl.ds(0, chunk)]
        loads.append(pltpu.make_async_copy(whole, whole, load_sem.at[number]))
    side_load = pltpu.make_async_copy(side_hbm, side, load_sem.at[3])
    side_load.start()
    adj_load = pltpu.make_async_copy(adj_hbm, adj, load_sem.at[4])
    adj_load.start()

    barrier = pltpu.get_barrier_semaphore()

    def member(number):
        return (group, number // (n_sub * n_cols), (number // n_sub) % n_cols, number % n_sub)

    def greet(step, carry):
        pl.semaphore_signal(
            barrier, inc=1, device_id=member((me + step) % members), device_id_type=MESH
        )
        return carry

    lax.fori_loop(1, members, greet, 0)

    def outside_rows(at):
        for ref in (ground, first, second, third):
            ref[pl.ds(at, DEPTH)] = jnp.full((DEPTH, SUBL, lanes), unreached, jnp.float32)

    pl.when(jnp.logical_not(has[-1]))(lambda: outside_rows(0))
    pl.when(jnp.logical_not(has[1]))(lambda: outside_rows(high))

    spans = {-1: (0, DEPTH), 0: (low, height), 1: (high, DEPTH)}
    for dc, ref in ((-1, ring_low), (1, ring_high)):
        for dr in (-1, 0, 1):

            def outside_ring(ref=ref, dr=dr):
                at, count = spans[dr]
                ref[:, pl.ds(at, count)] = jnp.full((2, count, 1, TILE), unreached, jnp.float32)

            pl.when(jnp.logical_not(both(dr, dc)))(outside_ring)

    adj_load.wait()
    lane_tile = lax.broadcasted_iota(jnp.int32, (n_tiles, padded), 1)
    linked = jnp.zeros((n_tiles, padded), jnp.float32)
    links = adj[...]
    for k in range(links.shape[1]):
        linked = jnp.where(links[:, k : k + 1] == lane_tile, 1.0, linked)
    own = lax.broadcasted_iota(jnp.int32, (n_tiles, padded), 0) == lane_tile
    linked = jnp.where(own, 1.0, linked)
    one_hop = linked
    if n_tiles < padded:
        one_hop = jnp.concatenate(
            [one_hop, jnp.zeros((padded - n_tiles, padded), jnp.float32)], axis=0
        )
    count = jnp.where(own, 0.0, 1.0)
    reach = linked
    for step in range(ROUNDS):
        count = count + (1.0 - reach)
        if step < ROUNDS - 1:
            reach = jnp.dot(reach, one_hop, preferred_element_type=jnp.float32)
            reach = jnp.where(reach > 0.5, 1.0, 0.0)
    hops[...] = count

    sub_id = lax.broadcasted_iota(jnp.int32, (SUBL, TILE), 0)
    lane_id = lax.broadcasted_iota(jnp.int32, (SUBL, TILE), 1)
    first_cell = jnp.logical_and(sub_id == 0, lane_id == 0)
    last_cell = jnp.logical_and(sub_id == SUBL - 1, lane_id == TILE - 1)
    is_first_col = (col == 0).astype(jnp.int32)
    is_last_col = (col == n_cols - 1).astype(jnp.int32)
    top_mark = jnp.where(band == 0, 1, 2)
    bottom_mark = jnp.where(band == bands - 1, 1, 2)
    right_half = lane_id < HALF

    def ring_of(ref, r):
        left_tile = ref[r, :, 0:TILE]
        right_tile = ref[r, :, chunk - TILE : chunk]
        return jnp.where(
            right_half, pltpu.roll(left_tile, SUBL - 1, 0), pltpu.roll(right_tile, 1, 0)
        )

    side_load.wait()
    for load in loads:
        load.wait()

    def start_row(i):
        height_row = ground[low + i, :, 0:chunk]
        water = height_row + fill[i]
        if i == 0:
            water = jnp.where(edge[0] == top_mark, height_row, water)
        if i == height - 1:
            water = jnp.where(edge[1] == bottom_mark, height_row, water)
        first[low + i, :, 0:chunk] = water
        mark = jnp.where(first_cell, side[0, i] * is_first_col, 0) == 1
        first[low + i, :, 0:TILE] = jnp.where(
            mark, ground[low + i, :, 0:TILE], first[low + i, :, 0:TILE]
        )
        at = chunk - TILE
        mark = jnp.where(last_cell, side[1, i] * is_last_col, 0) == 1
        first[low + i, :, at:chunk] = jnp.where(
            mark, ground[low + i, :, at:chunk], first[low + i, :, at:chunk]
        )
        for number, ref in enumerate((first, ground)):
            ring = ring_of(ref, low + i)
            ring_own[number, i] = ring
            ref[low + i, :, chunk:lanes] = ring

    order = [i for i in range(height) if i < DEPTH or i >= height - DEPTH]
    order += [i for i in range(height) if i not in order]
    for i in order:
        start_row(i)

    pl.semaphore_wait(barrier, members - 1)

    copies = []

    def send(src, dst, dr, dc):
        number = len(copies)
        copy = pltpu.make_async_remote_copy(
            src_ref=src,
            dst_ref=dst,
            send_sem=send_sem.at[number],
            recv_sem=recv_sem.at[number],
            device_id=device(dr, dc),
            device_id_type=MESH,
        )
        pl.when(both(dr, dc))(copy.start)
        copies.append((copy, dr, dc))
        return copy, dr, dc

    def arrive(entry):
        copy, dr, dc = entry
        pl.when(both(-dr, -dc))(copy.wait_recv)

    def rows_out(ref, dr, extent):
        src = low if dr == -1 else high - DEPTH
        dst = high if dr == -1 else 0
        return send(
            ref.at[pl.ds(src, DEPTH), :, pl.ds(0, extent)],
            ref.at[pl.ds(dst, DEPTH), :, pl.ds(0, extent)],
            dr, 0,
        )

    ring_in = []
    for dc in (-1, 1):
        for dr in (-1, 0, 1):
            at, count = {-1: (0, DEPTH), 0: (0, height), 1: (height - DEPTH, DEPTH)}[dr]
            to, _ = spans[-dr]
            target = ring_high if dc == -1 else ring_low
            part = SUBL - 1 if dc == -1 else 0
            ring_in.append(
                send(
                    ring_own.at[:, pl.ds(at, count), pl.ds(part, 1)],
                    target.at[:, pl.ds(to, count)],
                    dr, dc,
                )
            )
    row_in = {dr: [] for dr in (-1, 1)}
    for ref in (first, ground):
        for dr in (-1, 1):
            row_in[-dr].append(rows_out(ref, dr, chunk))

    def relax_rows(src, dst, r, count):
        rows = [src[r - 1 + i] for i in range(count + 2)]
        for i in range(count):
            above, here, below = rows[i : i + 3]
            low3 = jnp.minimum(jnp.minimum(above, below), here)
            least = jnp.minimum(
                low3, jnp.minimum(pltpu.roll(low3, 1, 1), pltpu.roll(low3, lanes - 1, 1))
            )
            value = jnp.maximum(ground[r + i], jnp.minimum(here, least + rise_step))
            if dst is done:
                done[r + i - low] = value[:, 0:chunk]
            else:
                dst[r + i] = value

    def inner(chain):
        for k in range(1, DEPTH + 1):
            src, dst = chain[k - 1], chain[k]
            begin, end = low + k, high - k

            def body(step, carry, src=src, dst=dst, begin=begin):
                relax_rows(src, dst, begin + 2 * step, 2)
                return carry

            lax.fori_loop(0, (end - begin) // 2, body, 0)

    def outer(chain, dr):
        for k in range(1, DEPTH + 1):
            begin = k if dr == -1 else high - k
            for i in range(0, DEPTH, 2):
                relax_rows(chain[k - 1], chain[k], begin + i, 2)

    def finish_ring(at, count):
        for r in range(at, at + count):
            for number, ref in enumerate((first, ground)):
                if at == low:
                    ring = ring_own[number, r - low]
                else:
                    ring = ring_of(ref, r)
                from_high = jnp.broadcast_to(ring_high[number, r], (SUBL, TILE))
                from_low = jnp.broadcast_to(ring_low[number, r], (SUBL, TILE))
                ring = jnp.where(
                    jnp.logical_and(sub_id == SUBL - 1, right_half), from_high, ring
                )
                ring = jnp.where(
                    jnp.logical_and(sub_id == 0, jnp.logical_not(right_half)), from_low, ring
                )
                ref[r, :, chunk:lanes] = ring

    for entry in ring_in:
        arrive(entry)
    finish_ring(low, height)
    chain = (first, ping, pong, ping, second)
    inner(chain)
    for dr, at in ((-1, 0), (1, high)):
        for entry in row_in[dr]:
            arrive(entry)
        finish_ring(at, DEPTH)
        outer(chain, dr)

    row_in = {-dr: rows_out(second, dr, lanes) for dr in (-1, 1)}
    chain = (second, ping, pong, ping, third)
    inner(chain)
    for dr in (-1, 1):
        arrive(row_in[dr])
        outer(chain, dr)

    row_in = {-dr: rows_out(third, dr, lanes) for dr in (-1, 1)}
    first_tile = third[low, :, 0:TILE]
    last_tile = third[low, :, chunk - TILE : chunk]
    for i in range(1, height):
        first_tile = jnp.minimum(first_tile, third[low + i, :, 0:TILE])
        last_tile = jnp.minimum(last_tile, third[low + i, :, chunk - TILE : chunk])
    floor = jnp.minimum(
        jnp.where(first_cell, first_tile, unreached), jnp.where(last_cell, last_tile, unreached)
    )
    for i, counts in ((low, sub == 0), (high - 1, sub == n_sub - 1)):
        skip = jnp.where(counts, -unreached, unreached)
        for j in range(chunk // TILE):
            floor = jnp.minimum(
                floor, jnp.maximum(third[i, :, j * TILE : (j + 1) * TILE], skip)
            )
    floor = jnp.min(floor, axis=(0, 1), keepdims=True)
    tile_id = tile_row * n_cols + col
    mine[...] = jnp.where(
        lax.broadcasted_iota(jnp.int32, (1, padded), 1) == tile_id,
        jnp.broadcast_to(floor, (1, padded)),
        unreached,
    )

    def level_copy(step):
        return pltpu.make_async_remote_copy(
            src_ref=mine,
            dst_ref=gathered.at[members - 1 - step],
            send_sem=level_send,
            recv_sem=level_recv,
            device_id=member((me + step) % members),
            device_id_type=MESH,
        )

    def spread(step, carry):
        level_copy(step).start()
        return carry

    lax.fori_loop(1, members, spread, 0)
    pltpu.make_async_copy(gathered, gathered, level_recv).wait()
    row = jnp.minimum(mine[...], jnp.min(gathered[...], axis=0))
    count = hops[...]
    best = jnp.full((n_tiles, padded), unreached, jnp.float32)
    for step in range(ROUNDS + 1):
        best = jnp.minimum(
            best, jnp.where(count == float(step), jnp.broadcast_to(row, best.shape), unreached)
        )
        row = row + hop_rise
    level = jnp.min(best, axis=1, keepdims=True)
    levels[...] = jnp.broadcast_to(level + spill_lift, levels.shape)

    def ceiling(row_at, col_at):
        at = jnp.clip(row_at, 0, n_rows - 1) * n_cols + jnp.clip(col_at, 0, n_cols - 1)
        return jnp.broadcast_to(levels[pl.ds(at, 1)], (SUBL, TILE))

    def clamp(at, count, row_at):
        here = ceiling(row_at, col)
        ring = jnp.where(
            jnp.logical_and(sub_id == SUBL - 1, right_half), ceiling(row_at, col + 1), here
        )
        ring = jnp.where(
            jnp.logical_and(sub_id == 0, jnp.logical_not(right_half)), ceiling(row_at, col - 1), ring
        )
        for r in range(at, at + count):
            for j in range(lanes // TILE):
                cut = slice(j * TILE, (j + 1) * TILE)
                top = ring if j == lanes // TILE - 1 else here
                pong[r, :, cut] = jnp.maximum(
                    ground[r, :, cut], jnp.minimum(third[r, :, cut], top)
                )

    clamp(low, height, tile_row)
    chain = (pong, ping, pong, ping, done)
    inner(chain)
    for dr, at in ((-1, 0), (1, high)):
        arrive(row_in[dr])
        clamp(at, DEPTH, (band + dr + n_sub) // n_sub - 1)
        outer(chain, dr)

    for s in range(SUBL):
        pltpu.make_async_copy(
            done.at[:, s], out_hbm.at[:, pl.ds(s * chunk, chunk)], out_sem
        ).start()
    for copy, dr, dc in copies:
        pl.when(both(dr, dc))(copy.wait_send)
    pltpu.make_async_copy(gathered, gathered, level_send).wait()
    pltpu.make_async_copy(done, done, out_sem).wait()


def per_device(sizes, elevation, fill_depth, edge_rows, edge_sides, adjacency):
    height, width = elevation.shape
    chunk = width // SUBL
    total = height + 2 * DEPTH
    members = sizes[1] * sizes[2] * sizes[3]
    n_tiles = adjacency.shape[0]
    padded = -(-n_tiles // TILE) * TILE
    wide = pltpu.VMEM((total, SUBL, chunk + TILE), jnp.float32)
    own = pltpu.VMEM((height, SUBL, chunk), jnp.float32)
    ring = pltpu.VMEM((2, total, 1, TILE), jnp.float32)
    return pl.pallas_call(
        functools.partial(kernel, sizes),
        out_shape=jax.ShapeDtypeStruct((height, width), jnp.float32),
        in_specs=[pl.BlockSpec(memory_space=pl.ANY)] * 5,
        out_specs=pl.BlockSpec(memory_space=pl.ANY),
        scratch_shapes=[
            wide, own, wide, wide, wide, wide, wide, own,
            pltpu.VMEM((2, SUBL, chunk), jnp.int32),
            pltpu.SMEM(edge_sides.shape, jnp.int32),
            pltpu.VMEM(adjacency.shape, jnp.int32),
            pltpu.VMEM((2, height, SUBL, TILE), jnp.float32),
            ring, ring,
            pltpu.VMEM((1, padded), jnp.float32),
            pltpu.VMEM((members - 1, 1, padded), jnp.float32),
            pltpu.VMEM((n_tiles, padded), jnp.float32),
            pltpu.VMEM((n_tiles, TILE), jnp.float32),
            pltpu.SemaphoreType.DMA((5,)),
            pltpu.SemaphoreType.DMA((14,)),
            pltpu.SemaphoreType.DMA((14,)),
            pltpu.SemaphoreType.DMA,
            pltpu.SemaphoreType.DMA,
            pltpu.SemaphoreType.DMA,
        ],
        compiler_params=pltpu.CompilerParams(
            collective_id=0, has_side_effects=True, vmem_limit_bytes=32 * 1024 * 1024
        ),
    )(elevation, fill_depth, edge_rows, edge_sides, adjacency)


def solution(mesh):
    sizes = tuple(mesh.shape[name] for name in ("groups", "rows", "cols", "sub"))
    placed = (
        P(("groups", "rows", "sub"), "cols"),
        P(("groups", "rows", "sub"), "cols"),
        P("groups", "cols"),
        P("groups", ("rows", "sub")),
        P("groups", None),
    )
    return jax.shard_map(
        functools.partial(per_device, sizes),
        mesh=mesh,
        in_specs=placed,
        out_specs=P(("groups", "rows", "sub"), "cols"),
        check_vma=False,
    )
```

time: 176 us -> 32.2 us (0.18)
  the two profiles are of different devices: /device:TPU:1 before, /device:TPU:0 now
where the time goes in v1:
time: 32.2 us; the launch traced here: 31.9 us
  Pallas kernels  26.8 us (83%)
  local copies, waits for them, and re-layouts  5.08 us (16%)
    pallas_call x1, Pallas kernels, per_device(): pl.pallas_call(functools.partial(kernel, sizes), out_shape=jax.ShapeDtype...  26.8 us
    unnamed x11, local copies, waits for them, and re-layouts  5.08 us

profile of v1, /device:TPU:0, one launch (start us, length us, event | category | flops | bytes accessed | tf_op | source)
XLA Modules:
  0.0 31.9 jit_solution(12930630120440331225)
XLA Ops:
  0.0 0.0 copy-start
  0.0 1.0 %copy-done = f32[16,8192]{1,0:T(8,128)S(1)} copy-done((f32[16,8192]{1,0:T(8,128)S(1)}, f32[16,8192]{1,0:T(8,128)}, u32[]{:S(2)}) %copy-start) | copy-done | bytes 524312
  1.0 0.0 copy-start.1
  1.0 1.0 %copy-done.1 = f32[16,8192]{1,0:T(8,128)S(1)} copy-done((f32[16,8192]{1,0:T(8,128)S(1)}, f32[16,8192]{1,0:T(8,128)}, u32[]{:S(2)}) %copy-start.1) | copy-done | bytes 524312
  2.1 0.0 copy-start.2
  2.1 0.8 %copy-done.2 = s32[2,8192]{1,0:T(2,128)S(1)} copy-done((s32[2,8192]{1,0:T(2,128)S(1)}, s32[2,8192]{1,0:T(2,128)}, u32[]{:S(2)}) %copy-start.2) | copy-done | bytes 65560
  2.9 0.0 copy-start.3
  2.9 0.7 %copy-done.3 = s32[8,6]{1,0:T(8,128)S(1)} copy-done((s32[8,6]{1,0:T(8,128)S(1)}, s32[8,6]{1,0:T(8,128)}, u32[]{:S(2)}) %copy-start.3) | copy-done | bytes 216
  3.6 0.0 copy-start.4
  3.6 0.7 %copy-done.4 = s32[2,16]{1,0:T(2,128)S(1)} copy-done((s32[2,16]{1,0:T(2,128)S(1)}, s32[2,16]{1,0:T(2,128)}, u32[]{:S(2)}) %copy-start.4) | copy-done | bytes 152
  4.3 26.8 %shard_map.55 = f32[16,8192]{1,0:T(8,128)S(1)} custom-call(f32[16,8192]{1,0:T(8,128)S(1)} %copy-done, f32[16,8192]{1,0:T(8,128)S(1)} %copy-done.1, s32[2,8192]{1,0:T(2,128)S(1)} %copy-done.2, s32[2,16]{1,0:T(2,128)S(1)} %copy-done.4, s32[8,6]{1,0:T(8,128)S(1)} %copy-done.3), custom_call_target="tpu_custom_call" | custom-call | tf_op jit(solution)/shard_map/pallas_call | solution.py:396
  31.1 0.8 %copy.7 = f32[16,8192]{1,0:T(8,128)} copy(f32[16,8192]{1,0:T(8,128)S(1)} %shard_map.55) | data formatting | bytes 1048576
Async XLA Ops:
  0.0 1.0 %copy-start = (f32[16,8192]{1,0:T(8,128)S(1)}, f32[16,8192]{1,0:T(8,128)}, u32[]{:S(2)}) copy-start(f32[16,8192]{1,0:T(8,128)} %elev_hbm.1) | copy-start | bytes 1572868
  1.0 1.0 %copy-start.1 = (f32[16,8192]{1,0:T(8,128)S(1)}, f32[16,8192]{1,0:T(8,128)}, u32[]{:S(2)}) copy-start(f32[16,8192]{1,0:T(8,128)} %fill_hbm.1) | copy-start | bytes 1572868
  2.1 0.8 %copy-start.2 = (s32[2,8192]{1,0:T(2,128)S(1)}, s32[2,8192]{1,0:T(2,128)}, u32[]{:S(2)}) copy-start(s32[2,8192]{1,0:T(2,128)} %edge_hbm.1) | copy-start | bytes 196612
  2.9 0.7 %copy-start.3 = (s32[8,6]{1,0:T(8,128)S(1)}, s32[8,6]{1,0:T(8,128)}, u32[]{:S(2)}) copy-start(s32[8,6]{1,0:T(8,128)} %adj_hbm.1) | copy-start | bytes 580
  3.6 0.7 %copy-start.4 = (s32[2,16]{1,0:T(2,128)S(1)}, s32[2,16]{1,0:T(2,128)}, u32[]{:S(2)}) copy-start(s32[2,16]{1,0:T(2,128)} %side_hbm.1) | copy-start | bytes 388

commit v2 on v1

--- a/solution.py
+++ b/solution.py
@@ -26,7 +26,7 @@
     sizes, elev_hbm, fill_hbm, edge_hbm, side_hbm, adj_hbm, out_hbm,
     ground, fill, first, second, third, ping, pong, done,
     edge, side, adj, ring_own, ring_low, ring_high,
-    mine, gathered, hops, levels,
+    mine, gathered, hops, levels, even, odd, seam_ground,
     load_sem, send_sem, recv_sem, level_send, level_recv, out_sem,
 ):
     n_groups, n_rows, n_cols, n_sub = sizes
@@ -47,19 +47,37 @@
     bands = n_rows * n_sub
     me = (tile_row * n_cols + col) * n_sub + sub
 
-    has = {-1: band > 0, 1: band < bands - 1, 0: True}
-    has_col = {-1: col > 0, 1: col < n_cols - 1, 0: True}
+    near = 1 - 2 * (band % 2)
+    far = -near
+
+    def has(dr):
+        return jnp.logical_and(band + dr >= 0, band + dr < bands)
+
+    has_col = {-1: col > 0, 1: col < n_cols - 1}
 
     def both(dr, dc):
-        if dr == 0:
+        if dc == 0:
+            return has(dr)
+        if isinstance(dr, int) and dr == 0:
             return has_col[dc]
-        if dc == 0:
-            return has[dr]
-        return jnp.logical_and(has[dr], has_col[dc])
+        return jnp.logical_and(has(dr), has_col[dc])
 
     def device(dr, dc):
         to_band = band + dr
         return (group, to_band // n_sub, col + dc, to_band % n_sub)
+
+    barrier = pltpu.get_barrier_semaphore()
+
+    def member(number):
+        return (group, number // (n_sub * n_cols), (number // n_sub) % n_cols, number % n_sub)
+
+    def greet(step, carry):
+        pl.semaphore_signal(
+            barrier, inc=1, device_id=member((me + step) % members), device_id_type=MESH
+        )
+        return carry
+
+    lax.fori_loop(1, members, greet, 0)
 
     loads = []
     for number, (src, dst, at) in enumerate(
@@ -79,25 +97,12 @@
     adj_load = pltpu.make_async_copy(adj_hbm, adj, load_sem.at[4])
     adj_load.start()
 
-    barrier = pltpu.get_barrier_semaphore()
-
-    def member(number):
-        return (group, number // (n_sub * n_cols), (number // n_sub) % n_cols, number % n_sub)
-
-    def greet(step, carry):
-        pl.semaphore_signal(
-            barrier, inc=1, device_id=member((me + step) % members), device_id_type=MESH
-        )
-        return carry
-
-    lax.fori_loop(1, members, greet, 0)
-
     def outside_rows(at):
         for ref in (ground, first, second, third):
             ref[pl.ds(at, DEPTH)] = jnp.full((DEPTH, SUBL, lanes), unreached, jnp.float32)
 
-    pl.when(jnp.logical_not(has[-1]))(lambda: outside_rows(0))
-    pl.when(jnp.logical_not(has[1]))(lambda: outside_rows(high))
+    pl.when(jnp.logical_not(has(-1)))(lambda: outside_rows(0))
+    pl.when(jnp.logical_not(has(1)))(lambda: outside_rows(high))
 
     spans = {-1: (0, DEPTH), 0: (low, height), 1: (high, DEPTH)}
     for dc, ref in ((-1, ring_low), (1, ring_high)):
@@ -197,13 +202,13 @@
         copies.append((copy, dr, dc))
         return copy, dr, dc
 
-    def arrive(entry):
+    def arrive(entry, mirrored):
         copy, dr, dc = entry
-        pl.when(both(-dr, -dc))(copy.wait_recv)
+        pl.when(both(-dr, -dc) if mirrored else both(dr, dc))(copy.wait_recv)
 
     def rows_out(ref, dr, extent):
-        src = low if dr == -1 else high - DEPTH
-        dst = high if dr == -1 else 0
+        src = jnp.where(dr < 0, low, high - DEPTH)
+        dst = jnp.where(dr < 0, high, 0)
         return send(
             ref.at[pl.ds(src, DEPTH), :, pl.ds(0, extent)],
             ref.at[pl.ds(dst, DEPTH), :, pl.ds(0, extent)],
@@ -224,10 +229,8 @@
                     dr, dc,
                 )
             )
-    row_in = {dr: [] for dr in (-1, 1)}
-    for ref in (first, ground):
-        for dr in (-1, 1):
-            row_in[-dr].append(rows_out(ref, dr, chunk))
+    sides = (near, far)
+    row_in = [[rows_out(ref, dr, chunk) for ref in (first, ground)] for dr in sides]
 
     def relax_rows(src, dst, r, count):
         rows = [src[r - 1 + i] for i in range(count + 2)]
@@ -245,57 +248,48 @@
 
     def inner(chain):
         for k in range(1, DEPTH + 1):
-            src, dst = chain[k - 1], chain[k]
-            begin, end = low + k, high - k
-
-            def body(step, carry, src=src, dst=dst, begin=begin):
-                relax_rows(src, dst, begin + 2 * step, 2)
-                return carry
-
-            lax.fori_loop(0, (end - begin) // 2, body, 0)
+            for r in range(low + k, high - k, 2):
+                relax_rows(chain[k - 1], chain[k], r, 2)
 
     def outer(chain, dr):
         for k in range(1, DEPTH + 1):
-            begin = k if dr == -1 else high - k
+            begin = jnp.where(dr < 0, k, high - k)
             for i in range(0, DEPTH, 2):
                 relax_rows(chain[k - 1], chain[k], begin + i, 2)
 
-    def finish_ring(at, count):
-        for r in range(at, at + count):
+    def finish_ring(at, count, own_rows):
+        for i in range(count):
+            r = at + i
             for number, ref in enumerate((first, ground)):
-                if at == low:
-                    ring = ring_own[number, r - low]
-                else:
-                    ring = ring_of(ref, r)
+                ring = ring_own[number, i] if own_rows else ring_of(ref, r)
                 from_high = jnp.broadcast_to(ring_high[number, r], (SUBL, TILE))
                 from_low = jnp.broadcast_to(ring_low[number, r], (SUBL, TILE))
-                ring = jnp.where(
-                    jnp.logical_and(sub_id == SUBL - 1, right_half), from_high, ring
-                )
-                ring = jnp.where(
-                    jnp.logical_and(sub_id == 0, jnp.logical_not(right_half)), from_low, ring
-                )
+                ring = jnp.where(at_high, from_high, jnp.where(at_low, from_low, ring))
                 ref[r, :, chunk:lanes] = ring
 
+    at_high = jnp.logical_and(sub_id == SUBL - 1, right_half)
+    at_low = jnp.logical_and(sub_id == 0, jnp.logical_not(right_half))
+
     for entry in ring_in:
-        arrive(entry)
-    finish_ring(low, height)
+        arrive(entry, True)
+    finish_ring(low, height, True)
     chain = (first, ping, pong, ping, second)
     inner(chain)
-    for dr, at in ((-1, 0), (1, high)):
-        for entry in row_in[dr]:
-            arrive(entry)
-        finish_ring(at, DEPTH)
+    row_next = []
+    for dr, entries in zip(sides, row_in):
+        for entry in entries:
+            arrive(entry, False)
+        finish_ring(jnp.where(dr < 0, 0, high), DEPTH, False)
         outer(chain, dr)
-
-    row_in = {-dr: rows_out(second, dr, lanes) for dr in (-1, 1)}
+        row_next.append(rows_out(second, dr, lanes))
+
+    row_in = row_next
     chain = (second, ping, pong, ping, third)
     inner(chain)
-    for dr in (-1, 1):
-        arrive(row_in[dr])
+    for dr, entry in zip(sides, row_in):
+        arrive(entry, False)
         outer(chain, dr)
 
-    row_in = {-dr: rows_out(third, dr, lanes) for dr in (-1, 1)}
     first_tile = third[low, :, 0:TILE]
     last_tile = third[low, :, chunk - TILE : chunk]
     for i in range(1, height):
@@ -333,6 +327,23 @@
         return carry
 
     lax.fori_loop(1, members, spread, 0)
+    row_in = [rows_out(third, dr, lanes) for dr in (far, near)][::-1]
+
+    chain = (third, ping, pong, ping, done)
+    inner(chain)
+    for dr, entry in zip(sides, row_in):
+        arrive(entry, False)
+        outer(chain, dr)
+
+    def seam_of(ref, r):
+        ring = ref[r, :, chunk:lanes]
+        at_first = jnp.where(right_half, ref[r, :, 0:TILE], ring)
+        at_last = jnp.where(right_half, ring, ref[r, :, chunk - TILE : chunk])
+        return jnp.where(sub_id == 0, at_first, at_last)
+
+    for r in range(total):
+        seam_ground[r] = seam_of(ground, r)
+
     pltpu.make_async_copy(gathered, gathered, level_recv).wait()
     row = jnp.minimum(mine[...], jnp.min(gathered[...], axis=0))
     count = hops[...]
@@ -349,29 +360,64 @@
         at = jnp.clip(row_at, 0, n_rows - 1) * n_cols + jnp.clip(col_at, 0, n_cols - 1)
         return jnp.broadcast_to(levels[pl.ds(at, 1)], (SUBL, TILE))
 
-    def clamp(at, count, row_at):
+    def ceilings(row_at):
         here = ceiling(row_at, col)
-        ring = jnp.where(
-            jnp.logical_and(sub_id == SUBL - 1, right_half), ceiling(row_at, col + 1), here
-        )
-        ring = jnp.where(
-            jnp.logical_and(sub_id == 0, jnp.logical_not(right_half)), ceiling(row_at, col - 1), ring
-        )
-        for r in range(at, at + count):
+        beside = jnp.where(
+            at_high, ceiling(row_at, col + 1), jnp.where(at_low, ceiling(row_at, col - 1), here)
+        )
+        return here, beside
+
+    above, own_row, below = (ceilings((band + dr + n_sub) // n_sub - 1) for dr in (-1, 0, 1))
+    beyond = ceilings((band + far + n_sub) // n_sub - 1)
+
+    seam = []
+    for r in range(total):
+        top = (above if r < low else own_row if r < high else below)[1]
+        seam.append(jnp.maximum(seam_ground[r], top))
+    for k in range(1, DEPTH + 1):
+        later = list(seam)
+        for r in range(k, total - k):
+            low3 = jnp.minimum(jnp.minimum(seam[r - 1], seam[r + 1]), seam[r])
+            least = jnp.minimum(
+                low3, jnp.minimum(pltpu.roll(low3, 1, 1), pltpu.roll(low3, TILE - 1, 1))
+            )
+            later[r] = jnp.maximum(seam_ground[r], jnp.minimum(seam[r], least + rise_step))
+        seam = later
+    for i in range(height):
+        seam_ground[low + i] = seam[low + i]
+
+    def flat(at, count, tops, targets):
+        here, beside = tops
+        for i in range(count):
             for j in range(lanes // TILE):
                 cut = slice(j * TILE, (j + 1) * TILE)
-                top = ring if j == lanes // TILE - 1 else here
-                pong[r, :, cut] = jnp.maximum(
-                    ground[r, :, cut], jnp.minimum(third[r, :, cut], top)
-                )
-
-    clamp(low, height, tile_row)
-    chain = (pong, ping, pong, ping, done)
-    inner(chain)
-    for dr, at in ((-1, 0), (1, high)):
-        arrive(row_in[dr])
-        clamp(at, DEPTH, (band + dr + n_sub) // n_sub - 1)
-        outer(chain, dr)
+                top = beside if j == lanes // TILE - 1 else here
+                value = jnp.maximum(ground[at + i, :, cut], top)
+                for target in targets:
+                    target[at + i, :, cut] = value
+
+    flat(jnp.where(far < 0, 0, high), DEPTH, beyond, (even,))
+    flat(jnp.where(far < 0, low, high - DEPTH - 1), DEPTH + 1, own_row, (even, odd))
+    outer((even, odd, even, odd, even), far)
+
+    left_seam = jnp.logical_and(sub_id == 0, lane_id < DEPTH)
+    right_seam = jnp.logical_and(sub_id == SUBL - 1, lane_id >= TILE - DEPTH)
+
+    def merge(at, count, is_far):
+        for i in range(count):
+            r = at + i
+            for j in range(chunk // TILE):
+                cut = slice(j * TILE, (j + 1) * TILE)
+                top = even[r, :, cut] if is_far else jnp.maximum(ground[r, :, cut], own_row[0])
+                value = jnp.minimum(done[r - low, :, cut], top)
+                if j == 0:
+                    value = jnp.where(left_seam, jnp.minimum(value, seam_ground[r]), value)
+                if j == chunk // TILE - 1:
+                    value = jnp.where(right_seam, jnp.minimum(value, seam_ground[r]), value)
+                done[r - low, :, cut] = value
+
+    merge(jnp.where(far < 0, low + DEPTH, low), height - DEPTH, False)
+    merge(jnp.where(far < 0, low, high - DEPTH), DEPTH, True)
 
     for s in range(SUBL):
         pltpu.make_async_copy(
@@ -396,7 +442,7 @@
     return pl.pallas_call(
         functools.partial(kernel, sizes),
         out_shape=jax.ShapeDtypeStruct((height, width), jnp.float32),
-        in_specs=[pl.BlockSpec(memory_space=pl.ANY)] * 5,
+        in_specs=[pl.BlockSpec(memory_space=pltpu.HBM)] * 5,
         out_specs=pl.BlockSpec(memory_space=pl.ANY),
         scratch_shapes=[
             wide, own, wide, wide, wide, wide, wide, own,
@@ -409,6 +455,8 @@
             pltpu.VMEM((members - 1, 1, padded), jnp.float32),
             pltpu.VMEM((n_tiles, padded), jnp.float32),
             pltpu.VMEM((n_tiles, TILE), jnp.float32),
+            wide, wide,
+            pltpu.VMEM((total, SUBL, TILE), jnp.float32),
             pltpu.SemaphoreType.DMA((5,)),
             pltpu.SemaphoreType.DMA((14,)),
             pltpu.SemaphoreType.DMA((14,)),

time: 32.2 us -> 27.1 us (0.84)
  the two profiles are of different devices: /device:TPU:0 before, /device:TPU:1 now
where the time goes in v2:
time: 27.1 us; the launch traced here: 26.8 us
  Pallas kernels  21.7 us (80%)
  local copies, waits for them, and re-layouts  5.08 us (19%)
    pallas_call x1, Pallas kernels, per_device(): pl.pallas_call(functools.partial(kernel, sizes), out_shape=jax.ShapeDtype...  21.7 us
    unnamed x11, local copies, waits for them, and re-layouts  5.08 us

profile of v2, /device:TPU:1, one launch (start us, length us, event | category | flops | bytes accessed | tf_op | source)
XLA Modules:
  0.0 26.8 jit_solution(13030118333912359689)
XLA Ops:
  0.0 0.0 copy-start
  0.0 1.0 %copy-done = f32[16,8192]{1,0:T(8,128)S(1)} copy-done((f32[16,8192]{1,0:T(8,128)S(1)}, f32[16,8192]{1,0:T(8,128)}, u32[]{:S(2)}) %copy-start) | copy-done | bytes 524312
  1.0 0.0 copy-start.1
  1.0 1.0 %copy-done.1 = f32[16,8192]{1,0:T(8,128)S(1)} copy-done((f32[16,8192]{1,0:T(8,128)S(1)}, f32[16,8192]{1,0:T(8,128)}, u32[]{:S(2)}) %copy-start.1) | copy-done | bytes 524312
  2.1 0.0 copy-start.2
  2.1 0.8 %copy-done.2 = s32[2,8192]{1,0:T(2,128)S(1)} copy-done((s32[2,8192]{1,0:T(2,128)S(1)}, s32[2,8192]{1,0:T(2,128)}, u32[]{:S(2)}) %copy-start.2) | copy-done | bytes 65560
  2.9 0.0 copy-start.3
  2.9 0.7 %copy-done.3 = s32[8,6]{1,0:T(8,128)S(1)} copy-done((s32[8,6]{1,0:T(8,128)S(1)}, s32[8,6]{1,0:T(8,128)}, u32[]{:S(2)}) %copy-start.3) | copy-done | bytes 216
  3.6 0.0 copy-start.4
  3.6 0.7 %copy-done.4 = s32[2,16]{1,0:T(2,128)S(1)} copy-done((s32[2,16]{1,0:T(2,128)S(1)}, s32[2,16]{1,0:T(2,128)}, u32[]{:S(2)}) %copy-start.4) | copy-done | bytes 152
  4.3 21.7 %shard_map.55 = f32[16,8192]{1,0:T(8,128)S(1)} custom-call(f32[16,8192]{1,0:T(8,128)S(1)} %copy-done, f32[16,8192]{1,0:T(8,128)S(1)} %copy-done.1, s32[2,8192]{1,0:T(2,128)S(1)} %copy-done.2, s32[2,16]{1,0:T(2,128)S(1)} %copy-done.4, s32[8,6]{1,0:T(8,128)S(1)} %copy-done.3), custom_call_target="tpu_custom_call" | custom-call | tf_op jit(solution)/shard_map/pallas_call | solution.py:442
  26.0 0.8 %copy.7 = f32[16,8192]{1,0:T(8,128)} copy(f32[16,8192]{1,0:T(8,128)S(1)} %shard_map.55) | data formatting | bytes 1048576
Async XLA Ops:
  0.0 1.0 %copy-start = (f32[16,8192]{1,0:T(8,128)S(1)}, f32[16,8192]{1,0:T(8,128)}, u32[]{:S(2)}) copy-start(f32[16,8192]{1,0:T(8,128)} %elev_hbm.1) | copy-start | bytes 1572868
  1.0 1.0 %copy-start.1 = (f32[16,8192]{1,0:T(8,128)S(1)}, f32[16,8192]{1,0:T(8,128)}, u32[]{:S(2)}) copy-start(f32[16,8192]{1,0:T(8,128)} %fill_hbm.1) | copy-start | bytes 1572868
  2.1 0.8 %copy-start.2 = (s32[2,8192]{1,0:T(2,128)S(1)}, s32[2,8192]{1,0:T(2,128)}, u32[]{:S(2)}) copy-start(s32[2,8192]{1,0:T(2,128)} %edge_hbm.1) | copy-start | bytes 196612
  2.9 0.7 %copy-start.3 = (s32[8,6]{1,0:T(8,128)S(1)}, s32[8,6]{1,0:T(8,128)}, u32[]{:S(2)}) copy-start(s32[8,6]{1,0:T(8,128)} %adj_hbm.1) | copy-start | bytes 580
  3.6 0.7 %copy-start.4 = (s32[2,16]{1,0:T(2,128)S(1)}, s32[2,16]{1,0:T(2,128)}, u32[]{:S(2)}) copy-start(s32[2,16]{1,0:T(2,128)} %side_hbm.1) | copy-start | bytes 388

commit v3 on v2

--- a/solution.py
+++ b/solution.py
@@ -114,28 +114,6 @@
 
             pl.when(jnp.logical_not(both(dr, dc)))(outside_ring)
 
-    adj_load.wait()
-    lane_tile = lax.broadcasted_iota(jnp.int32, (n_tiles, padded), 1)
-    linked = jnp.zeros((n_tiles, padded), jnp.float32)
-    links = adj[...]
-    for k in range(links.shape[1]):
-        linked = jnp.where(links[:, k : k + 1] == lane_tile, 1.0, linked)
-    own = lax.broadcasted_iota(jnp.int32, (n_tiles, padded), 0) == lane_tile
-    linked = jnp.where(own, 1.0, linked)
-    one_hop = linked
-    if n_tiles < padded:
-        one_hop = jnp.concatenate(
-            [one_hop, jnp.zeros((padded - n_tiles, padded), jnp.float32)], axis=0
-        )
-    count = jnp.where(own, 0.0, 1.0)
-    reach = linked
-    for step in range(ROUNDS):
-        count = count + (1.0 - reach)
-        if step < ROUNDS - 1:
-            reach = jnp.dot(reach, one_hop, preferred_element_type=jnp.float32)
-            reach = jnp.where(reach > 0.5, 1.0, 0.0)
-    hops[...] = count
-
     sub_id = lax.broadcasted_iota(jnp.int32, (SUBL, TILE), 0)
     lane_id = lax.broadcasted_iota(jnp.int32, (SUBL, TILE), 1)
     first_cell = jnp.logical_and(sub_id == 0, lane_id == 0)
@@ -269,6 +247,28 @@
 
     at_high = jnp.logical_and(sub_id == SUBL - 1, right_half)
     at_low = jnp.logical_and(sub_id == 0, jnp.logical_not(right_half))
+
+    adj_load.wait()
+    lane_tile = lax.broadcasted_iota(jnp.int32, (n_tiles, padded), 1)
+    linked = jnp.zeros((n_tiles, padded), jnp.float32)
+    links = adj[...]
+    for k in range(links.shape[1]):
+        linked = jnp.where(links[:, k : k + 1] == lane_tile, 1.0, linked)
+    own = lax.broadcasted_iota(jnp.int32, (n_tiles, padded), 0) == lane_tile
+    linked = jnp.where(own, 1.0, linked)
+    one_hop = linked
+    if n_tiles < padded:
+        one_hop = jnp.concatenate(
+            [one_hop, jnp.zeros((padded - n_tiles, padded), jnp.float32)], axis=0
+        )
+    count = jnp.where(own, 0.0, 1.0)
+    reach = linked
+    for step in range(ROUNDS):
+        count = count + (1.0 - reach)
+        if step < ROUNDS - 1:
+            reach = jnp.dot(reach, one_hop, preferred_element_type=jnp.float32)
+            reach = jnp.where(reach > 0.5, 1.0, 0.0)
+    hops[...] = count
 
     for entry in ring_in:
         arrive(entry, True)

time: 27.1 us -> 27.1 us (level)
  no operation moved by 1% of the time
where the time goes in v3:
time: 27.1 us; the launch traced here: 26.8 us
  Pallas kernels  21.7 us (80%)
  local copies, waits for them, and re-layouts  5.08 us (19%)
    pallas_call x1, Pallas kernels, per_device(): pl.pallas_call(functools.partial(kernel, sizes), out_shape=jax.ShapeDtype...  21.7 us
    unnamed x11, local copies, waits for them, and re-layouts  5.08 us

profile of v3, /device:TPU:1, one launch (start us, length us, event | category | flops | bytes accessed | tf_op | source)
XLA Modules:
  0.0 26.8 jit_solution(5709247194305535473)
XLA Ops:
  0.0 0.0 copy-start
  0.0 1.0 %copy-done = f32[16,8192]{1,0:T(8,128)S(1)} copy-done((f32[16,8192]{1,0:T(8,128)S(1)}, f32[16,8192]{1,0:T(8,128)}, u32[]{:S(2)}) %copy-start) | copy-done | bytes 524312
  1.0 0.0 copy-start.1
  1.0 1.0 %copy-done.1 = f32[16,8192]{1,0:T(8,128)S(1)} copy-done((f32[16,8192]{1,0:T(8,128)S(1)}, f32[16,8192]{1,0:T(8,128)}, u32[]{:S(2)}) %copy-start.1) | copy-done | bytes 524312
  2.1 0.0 copy-start.2
  2.1 0.8 %copy-done.2 = s32[2,8192]{1,0:T(2,128)S(1)} copy-done((s32[2,8192]{1,0:T(2,128)S(1)}, s32[2,8192]{1,0:T(2,128)}, u32[]{:S(2)}) %copy-start.2) | copy-done | bytes 65560
  2.9 0.0 copy-start.3
  2.9 0.7 %copy-done.3 = s32[8,6]{1,0:T(8,128)S(1)} copy-done((s32[8,6]{1,0:T(8,128)S(1)}, s32[8,6]{1,0:T(8,128)}, u32[]{:S(2)}) %copy-start.3) | copy-done | bytes 216
  3.6 0.0 copy-start.4
  3.6 0.7 %copy-done.4 = s32[2,16]{1,0:T(2,128)S(1)} copy-done((s32[2,16]{1,0:T(2,128)S(1)}, s32[2,16]{1,0:T(2,128)}, u32[]{:S(2)}) %copy-start.4) | copy-done | bytes 152
  4.3 21.7 %shard_map.55 = f32[16,8192]{1,0:T(8,128)S(1)} custom-call(f32[16,8192]{1,0:T(8,128)S(1)} %copy-done, f32[16,8192]{1,0:T(8,128)S(1)} %copy-done.1, s32[2,8192]{1,0:T(2,128)S(1)} %copy-done.2, s32[2,16]{1,0:T(2,128)S(1)} %copy-done.4, s32[8,6]{1,0:T(8,128)S(1)} %copy-done.3), custom_call_target="tpu_custom_call" | custom-call | tf_op jit(solution)/shard_map/pallas_call | solution.py:442
  26.0 0.8 %copy.7 = f32[16,8192]{1,0:T(8,128)} copy(f32[16,8192]{1,0:T(8,128)S(1)} %shard_map.55) | data formatting | bytes 1048576
Async XLA Ops:
  0.0 1.0 %copy-start = (f32[16,8192]{1,0:T(8,128)S(1)}, f32[16,8192]{1,0:T(8,128)}, u32[]{:S(2)}) copy-start(f32[16,8192]{1,0:T(8,128)} %elev_hbm.1) | copy-start | bytes 1572868
  1.0 1.0 %copy-start.1 = (f32[16,8192]{1,0:T(8,128)S(1)}, f32[16,8192]{1,0:T(8,128)}, u32[]{:S(2)}) copy-start(f32[16,8192]{1,0:T(8,128)} %fill_hbm.1) | copy-start | bytes 1572868
  2.1 0.8 %copy-start.2 = (s32[2,8192]{1,0:T(2,128)S(1)}, s32[2,8192]{1,0:T(2,128)}, u32[]{:S(2)}) copy-start(s32[2,8192]{1,0:T(2,128)} %edge_hbm.1) | copy-start | bytes 196612
  2.9 0.7 %copy-start.3 = (s32[8,6]{1,0:T(8,128)S(1)}, s32[8,6]{1,0:T(8,128)}, u32[]{:S(2)}) copy-start(s32[8,6]{1,0:T(8,128)} %adj_hbm.1) | copy-start | bytes 580
  3.6 0.7 %copy-start.4 = (s32[2,16]{1,0:T(2,128)S(1)}, s32[2,16]{1,0:T(2,128)}, u32[]{:S(2)}) copy-start(s32[2,16]{1,0:T(2,128)} %side_hbm.1) | copy-start | bytes 388
